TPU v7x, 32 devices: a whole 2x2x4 slice. The times are simulated.
32 devices in a mesh: pert: 8 (over y, x, core), gx: 4 (over z).
Axes of the slice: x: 2, y: 2, z: 4, core: 2. Of those that a mesh axis runs over, the one named last changes fastest.
Arguments:
- pert_field: float32 [8, 3, 1024, 8, 1024], P('pert', None, 'gx'), may hold values from -6 to 6
- base_store: bfloat16 [8, 3, 1024, 8, 1024], P('pert', None, 'gx'), may hold values from -6 to 6
- section_owner: int32 [1], replicated, may hold values from 0 to 7
- pert_ids: int32 [8], P('pert'), may hold values from 0 to 63
- member_visc: float32 [64], replicated, may hold values from 0.05 to 0.5
Outputs:
- section_field: float32 [8, 3, 1024, 2, 1024], P('pert', None, 'gx')
All inputs are finite; a program needn't handle non-finite values.
Results may differ from a plain program's by a relative error of at most 0.0003.
Values may be sent and summed in bfloat16 or wider, within the bound.
No kernel may reach another device: no remote copies, remote signals or barrier semaphores. Data moves between devices by JAX's collectives and lax.ppermute only.
A program may use at most 320 MiB of HBM per device.

v0:
```python
import math
import jax
import jax.numpy as jnp
from jax import lax
from jax.sharding import PartitionSpec as P

first_weights = (0.75, -0.15, 1.0 / 60.0)
second_weights = (1.5, -0.15, 1.0 / 90.0)
centre_second = -49.0 / 18.0
section_step = 0.25


def extended(array, sides, width):
    for axis, dim in sides:
        size, length = (lax.axis_size(axis), array.shape[dim])
        up = [(i, (i + 1) % size) for i in range(size)]
        down = [(j, i) for i, j in up]
        last = lax.slice_in_dim(array, length - width, length, axis=dim)
        first = lax.slice_in_dim(array, 0, width, axis=dim)
        before = lax.ppermute(last, axis, up)
        after = lax.ppermute(first, axis, down)
        array = jnp.concatenate([before, array, after], axis=dim)
    return array


def broadcast(value, axis, source):
    kept = jnp.where(lax.axis_index(axis) == source, value, 0).astype(value.dtype)
    return lax.psum(kept, axis)


def first_across(values, axis_number):
    summed = jnp.zeros_like(values)
    for offset_cells, weight in zip((1, 2, 3), first_weights):
        summed = summed + weight * (
            jnp.roll(values, -offset_cells, axis_number)
            - jnp.roll(values, offset_cells, axis_number)
        )
    return summed


def second_across(values, axis_number):
    summed = centre_second * values
    for offset_cells, weight in zip((1, 2, 3), second_weights):
        summed = summed + weight * (
            jnp.roll(values, -offset_cells, axis_number)
            + jnp.roll(values, offset_cells, axis_number)
        )
    return summed


def first_depth(values, plane_count):
    summed = jnp.zeros_like(values[:, :, 3 : 3 + plane_count])
    for offset_cells, weight in zip((1, 2, 3), first_weights):
        summed = summed + weight * (
            values[:, :, 3 + offset_cells : 3 + offset_cells + plane_count]
            - values[:, :, 3 - offset_cells : 3 - offset_cells + plane_count]
        )
    return summed


def second_depth(values, plane_count):
    summed = centre_second * values[:, :, 3 : 3 + plane_count]
    for offset_cells, weight in zip((1, 2, 3), second_weights):
        summed = summed + weight * (
            values[:, :, 3 + offset_cells : 3 + offset_cells + plane_count]
            + values[:, :, 3 - offset_cells : 3 - offset_cells + plane_count]
        )
    return summed


def local_inverse(slab_width):
    counter = jnp.arange(1, slab_width + 1, dtype=jnp.int32)
    period = 2 * (slab_width + 1)
    product_index = counter[:, None] * counter[None, :] % period
    sine_angle = math.pi / (slab_width + 1)
    sine_basis = jnp.sin(sine_angle * product_index.astype(jnp.float32)) * math.sqrt(
        2.0 / (slab_width + 1)
    )
    eigenvalues = 1.0 + 2.0 / 3.0 * jnp.cos(sine_angle * counter.astype(jnp.float32))
    return jnp.dot(sine_basis / eigenvalues[None, :], sine_basis, precision=lax.Precision.HIGHEST)


def along_terms(pert_interior, base_interior, inverse):
    stacked_rims = jnp.concatenate([pert_interior, base_interior], 0)
    padded_rims = extended(stacked_rims, (("gx", 1),), 3)
    slab_width = pert_interior.shape[1]

    def shifted(offset_cells):
        return padded_rims[:, 3 + offset_cells : 3 + offset_cells + slab_width]

    compact_rhs = 7.0 / 9.0 * (shifted(1) - shifted(-1)) + 1.0 / 36.0 * (shifted(2) - shifted(-2))
    particular = jnp.einsum("ij,cjzy->cizy", inverse, compact_rhs, precision=lax.Precision.HIGHEST)
    padded_solve = extended(particular.astype(jnp.bfloat16), (("gx", 1),), 1).astype(
        particular.dtype
    )
    left_last = padded_solve[:, 0]
    right_first = padded_solve[:, slab_width + 1]
    coupling = inverse[0, 0] / 3.0
    coupling_gain = 1.0 / (1.0 - coupling * coupling)
    left_value = (left_last - coupling * particular[:, 0]) * coupling_gain
    right_value = (right_first - coupling * particular[:, slab_width - 1]) * coupling_gain
    correction = (
        inverse[:, 0][None, :, None, None] * left_value[:, None]
        + inverse[:, slab_width - 1][None, :, None, None] * right_value[:, None]
    )
    derivative = particular - correction / 3.0
    pert_curve = centre_second * shifted(0)[:3]
    for offset_cells, weight in zip((1, 2, 3), second_weights):
        pert_curve = pert_curve + weight * (shifted(offset_cells)[:3] + shifted(-offset_cells)[:3])
    return (derivative[:3], pert_curve, derivative[3:])


def per_device(pert_field, base_store, section_owner, pert_ids, member_visc):
    state_field = pert_field[0]
    plane_count = state_field.shape[2] - 6
    interior = state_field[:, :, 3 : 3 + plane_count]
    inverse = local_inverse(state_field.shape[1])
    member_count = member_visc.shape[0]
    member_pick = (pert_ids[0] == jnp.arange(member_count, dtype=jnp.int32)).astype(jnp.float32)
    viscosity = jnp.sum(member_pick * member_visc)
    owner_level = section_owner[0]
    levels_here = base_store.shape[0]
    owner_slot = owner_level % levels_here
    owner_root = owner_level // levels_here
    stored_tile = lax.dynamic_index_in_dim(base_store, owner_slot, 0, keepdims=False)
    base_field = broadcast(stored_tile, "pert", owner_root).astype(jnp.float32)
    base_interior = base_field[:, :, 3 : 3 + plane_count]
    pert_along, pert_curve, base_along = along_terms(interior, base_interior, inverse)
    base_across = first_across(base_interior, 3)
    base_depth = first_depth(base_field, plane_count)
    pert_across = first_across(interior, 3)
    pert_depth = first_depth(state_field, plane_count)
    laplacian = pert_curve + second_across(interior, 3) + second_depth(state_field, plane_count)
    advection = (
        base_interior[0] * pert_along
        + base_interior[1] * pert_across
        + base_interior[2] * pert_depth
    )
    stretching = interior[0] * base_along + interior[1] * base_across + interior[2] * base_depth
    updated = interior + section_step * (-advection - stretching + viscosity * laplacian)
    return updated[None]


def solution(mesh):
    placed = (
        P("pert", None, "gx", None, None),
        P("pert", None, "gx", None, None),
        P(),
        P("pert"),
        P(),
    )
    return jax.shard_map(
        per_device,
        mesh=mesh,
        in_specs=placed,
        out_specs=P("pert", None, "gx", None, None),
        check_vma=False,
    )
```

profile of v0, /device:TPU:0, one launch (start us, length us, event | category | flops | bytes accessed | tf_op | source)
XLA Modules:
  0.0 418.0 jit_solution(17584555150854972511)
XLA Ops:
  7.2 23.5 %fusion.8 = bf16[3,256,8,1024]{3,1,2,0:T(8,128)(2,1)} fusion(bf16[1,3,256,8,1024]{4,3,2,1,0:T(8,128)(2,1)} %param.6, pred[]{:T(512)S(6)} %eq.13), kind=kLoop, calls=%fused_computation.12 | loop fusion | flops 6291456 | bytes 25165824 | tf_op jit(solution)/shard_map/jit(_where)/select_n | solution.py:27
  30.8 21.9 %copy.20 = f32[1,3,256,8,1024]{4,2,3,1,0:T(8,128)S(1)} copy(f32[1,3,256,8,1024]{4,3,2,1,0:T(8,128)} %param.5) | data formatting | bytes 50331648 | tf_op args[0]
  52.7 3.7 slice.347
  56.4 2.6 fusion.47
  59.1 1.3 slice.357
  63.6 1.5 fusion.83
  65.0 1.5 fusion.81
  66.5 1.4 fusion.79
  68.0 2.8 slice_bitcast_fusion.2
  70.8 11.5 %fusion.82 = (f32[3,256,2,1021]{3,1,2,0:T(8,128)}, f32[3,256,2,1021]{3,1,2,0:T(8,128)}) fusion(f32[3,256,8,1024]{3,1,2,0:T(8,128)} %bitcast.43), kind=kLoop, calls=%fused_computation.120 | loop fusion | bytes 25092096 | tf_op jit(solution)/shard_map/jit(_roll_static)/slice | solution.py:35
  82.3 11.3 %fusion.80 = (f32[3,256,2,1022]{3,1,2,0:T(8,128)}, f32[3,256,2,1022]{3,1,2,0:T(8,128)}) fusion(f32[3,256,8,1024]{3,1,2,0:T(8,128)} %bitcast.44), kind=kLoop, calls=%fused_computation.118 | loop fusion | bytes 25116672 | tf_op jit(solution)/shard_map/jit(_roll_static)/slice | solution.py:35
  93.5 11.1 %fusion.78 = (f32[3,256,2,1023]{3,1,2,0:T(8,128)}, f32[3,256,2,1023]{3,1,2,0:T(8,128)}) fusion(f32[3,256,8,1024]{3,1,2,0:T(8,128)} %bitcast.45), kind=kLoop, calls=%fused_computation.116 | loop fusion | bytes 25141248 | tf_op jit(solution)/shard_map/jit(_roll_static)/slice | solution.py:35
  104.6 101.3 %all-reduce.2.cloned.1.call-done = bf16[3,256,8,1024]{3,1,2,0:T(8,128)(2,1)} async-done(((bf16[3,256,8,1024]{3,1,2,0:T(8,128)(2,1)}), bf16[3,256,8,1024]{3,1,2,0:T(8,128)(2,1)}) %all-reduce.2.cloned.1.call-update) | async-done | bytes 12582928 | tf_op jit(solution)/shard_map/psum | solution.py:28
  205.9 2.8 slice.349
  208.7 4.5 %pad_maximum_fusion.8 = (f32[6,3,2,1024]{3,1,2,0:T(4,128)}, f32[6,3,2,1024]{3,1,2,0:T(4,128)}) fusion(f32[3,256,2,1024]{3,1,2,0:T(8,128)S(1)} %slice.349, f32[3,256,2,1024]{3,1,2,0:T(8,128)} %slice.347), kind=kLoop, calls=%fused_computation.87 | loop fusion | flops 73728 | bytes 12877824 | tf_op jit(solution)/shard_map/slice | solution.py:19
  213.2 3.6 collective-permute-start
  216.8 8.8 %convert_element_type.24 = f32[3,256,8,1024]{3,1,2,0:T(8,128)} convert(bf16[3,256,8,1024]{3,1,2,0:T(8,128)(2,1)S(1)} %bitcast.48) | non-fusion elementwise | flops 6291456 | bytes 37748736 | tf_op jit(solution)/shard_map/convert_element_type | solution.py:126
  225.6 5.7 %slice_bitcast_fusion.5 = (f32[256,2,1024]{2,0,1:T(8,128)}, f32[256,2,1024]{2,0,1:T(8,128)}, f32[256,2,1024]{2,0,1:T(8,128)}) fusion(f32[3,256,8,1024]{3,1,2,0:T(8,128)} %convert_element_type.24), kind=kLoop, calls=%fused_computation.73 | loop fusion | bytes 12582912 | tf_op jit(solution)/shard_map/mul | solution.py:135
  231.3 1.3 fusion.88
  232.6 6.4 %fusion.89 = (f32[3,256,2,1023]{3,1,2,0:T(8,128)}, f32[3,256,2,1023]{3,1,2,0:T(8,128)}) fusion(bf16[3,256,8,1024]{3,1,2,0:T(8,128)(2,1)S(1)} %bitcast.48), kind=kLoop, calls=%fused_computation.127 | loop fusion | bytes 25141248 | tf_op jit(solution)/shard_map/jit(_roll_static)/slice | solution.py:36
  239.0 6.3 %fusion.87 = (f32[3,256,2,1022]{3,1,2,0:T(8,128)}, f32[3,256,2,1022]{3,1,2,0:T(8,128)}) fusion(bf16[3,256,8,1024]{3,1,2,0:T(8,128)(2,1)S(1)} %bitcast.48), kind=kLoop, calls=%fused_computation.125 | loop fusion | bytes 25116672 | tf_op jit(solution)/shard_map/jit(_roll_static)/slice | solution.py:36
  245.3 6.3 %fusion.85 = (f32[3,256,2,1021]{3,1,2,0:T(8,128)}, f32[3,256,2,1021]{3,1,2,0:T(8,128)}) fusion(bf16[3,256,8,1024]{3,1,2,0:T(8,128)(2,1)S(1)} %bitcast.48), kind=kLoop, calls=%fused_computation.123 | loop fusion | bytes 25092096 | tf_op jit(solution)/shard_map/jit(_roll_static)/slice | solution.py:36
  251.6 1.4 fusion.86
  253.0 14.4 %pad_maximum_fusion = (f32[6,259,2,1024]{3,1,2,0:T(8,128)}, f32[6,259,2,1024]{3,1,2,0:T(8,128)}) fusion(f32[6,3,2,1024]{3,1,2,0:T(4,128)S(1)} %collective-permute-done, f32[3,256,2,1024]{3,1,2,0:T(8,128)} %copy-done.1, f32[3,256,2,1024]{3,1,2,0:T(8,128)S(1)} %bitcast.50, f32[6,3,2,1024]{3,1,2,0:T(4,128)S(1)} %collective-permute-done.1), kind=kLoop, calls=%fused_computation.1 | loop fusion | flops 12730368 | bytes 38338560 | tf_op jit(solution)/shard_map/concatenate | solution.py:22
  267.4 37.6 %fusion.92 = (bf16[6,256,2,1024]{3,1,2,0:T(8,128)(2,1)}, f32[6,256,2,1024]{3,1,2,0:T(8,128)}) fusion(f32[256,256]{0,1:T(8,128)} %copy-done.2, f32[6,259,2,1024]{3,1,2,0:T(8,128)} %get-tuple-element.38, f32[6,259,2,1024]{3,1,2,0:T(8,128)} %get-tuple-element.37), kind=kOutput, calls=%fused_computation.130 | convolution fusion | flops 9682550784 | bytes 69468160 | tf_op jit(solution)/shard_map/ij,cjzy->cizy/dot_general | solution.py:92
  306.1 3.9 collective-permute-start.3
  309.9 2.5 fusion.84
  312.5 3.4 collective-permute-done.2
  315.8 1.3 fusion.69
  317.2 12.4 %multiply_subtract_fusion = f32[6,256,2,1024]{3,1,2,0:T(8,128)} fusion(f32[6,256,2,1024]{3,1,2,0:T(8,128)} %get-tuple-element.46, f32[6,2,1024]{2,1,0:T(2,128)S(1)} %get-tuple-element.47, f32[256]{0:T(256)S(1)} %bitcast.52, f32[6,2,1024]{2,1,0:T(2,128)S(1)} %get-tuple-element.48, f32[256]{0:T(256)S(1)} %bitcast.51), kind=kLoop, calls=%fused_computation.13 | loop fusion | flops 15728640 | bytes 25266176 | tf_op jit(solution)/shard_map/sub | solution.py:106
  329.6 73.8 %fusion.17 = f32[1,3,256,2,1024]{4,2,3,1,0:T(8,128)S(1)} fusion(f32[6,259,2,1024]{3,1,2,0:T(8,128)} %get-tuple-element.38, f32[6,259,2,1024]{3,1,2,0:T(8,128)} %get-tuple-element.37, f32[3,256,8,1024]{3,1,2,0:T(8,128)} %convert_element_type.24, f32[6,256,2,1024]{3,1,2,0:T(8,128)} %multiply_subtract_fusion, f32[3,256,2,1]{3,1,2,0:T(8,128)} %get-tuple-element.34, ...), kind=kLoop, calls=%fused_computation.23 | loop fusion | flops 141557760 | bytes 226492416 | tf_op jit(solution)/shard_map/broadcast_in_dim | solution.py:141
  403.4 7.6 %copy.9 = f32[1,3,256,2,1024]{4,3,2,1,0:T(2,128)} copy(f32[1,3,256,2,1024]{4,2,3,1,0:T(8,128)S(1)} %fusion.17) | data formatting | bytes 12582912 | tf_op jit(solution)/shard_map/broadcast_in_dim | solution.py:141
  (33 shorter events, 1.9 us)
Async XLA Ops:
  6.5 199.4 %all-reduce.2.cloned.1.call-start = ((), (), s32[]{:S(2)}) async-start(), calls=%async_computation | async-start | bytes 25165824 | tf_op jit(solution)/shard_map/psum | solution.py:28
  52.7 15.3 %copy-start = (f32[1,3,256,8,1024]{4,2,3,1,0:T(8,128)}, f32[1,3,256,8,1024]{4,2,3,1,0:T(8,128)S(1)}, u32[]{:S(2)}) copy-start(f32[1,3,256,8,1024]{4,2,3,1,0:T(8,128)S(1)} %copy.20) | copy-start | bytes 75497472
  52.7 10.2 %copy-start.3 = (f32[64]{0:T(128)S(1)}, f32[64]{0:T(128)}, u32[]{:S(2)}) copy-start(f32[64]{0:T(128)} %param.9) | copy-start | bytes 772
  59.1 4.5 %copy-start.2 = (f32[256,256]{0,1:T(8,128)}, f32[256,256]{0,1:T(8,128)S(1)}, u32[]{:S(2)}) copy-start(f32[256,256]{0,1:T(8,128)S(1)} %fusion.47) | copy-start | bytes 786436
  205.9 10.9 %slice-start = ((s8[12582912]{0:T(1024)(128)(4,1)}), s8[4194304]{0:T(1024)(128)(4,1)S(1)}, s32[]{:S(2)}) async-start(s8[12582912]{0:T(1024)(128)(4,1)} %bitcast.47), calls=%async_computation.1 | async-start | bytes 8388608
  205.9 10.9 %slice-start.1 = ((s8[12582912]{0:T(1024)(128)(4,1)}), s8[4194304]{0:T(1024)(128)(4,1)S(1)}, s32[]{:S(2)}) async-start(s8[12582912]{0:T(1024)(128)(4,1)} %bitcast.47), calls=%async_computation.2 | async-start | bytes 8388608
  208.7 4.5 %copy-start.1 = (f32[3,256,2,1024]{3,1,2,0:T(8,128)}, f32[3,256,2,1024]{3,1,2,0:T(8,128)S(1)}, u32[]{:S(2)}) copy-start(f32[3,256,2,1024]{3,1,2,0:T(8,128)S(1)} %slice.349) | copy-start | bytes 18874372
  208.7 8.1 %slice-start.2 = ((s8[12582912]{0:T(1024)(128)(4,1)}), s8[4194304]{0:T(1024)(128)(4,1)S(1)}, s32[]{:S(2)}) async-start(s8[12582912]{0:T(1024)(128)(4,1)} %bitcast.47), calls=%async_computation.3 | async-start | bytes 8388608
  213.2 39.7 %collective-permute-start = (f32[6,3,2,1024]{3,1,2,0:T(4,128)}, f32[6,3,2,1024]{3,1,2,0:T(4,128)S(1)}, u32[]{:S(2)}, u32[]{:S(2)}) collective-permute-start(f32[6,3,2,1024]{3,1,2,0:T(4,128)} %get-tuple-element.39), channel_id=1, source_target_pairs={{1,0},{2,1},{3,2},{0,3},{5,4},{6,5},{7,6},{4,7},{9,8},{10,9},{11,1... | collective-permute-start | bytes 442376 | tf_op jit(solution)/shard_map/ppermute | solution.py:21
  216.8 36.2 %collective-permute-start.1 = (f32[6,3,2,1024]{3,1,2,0:T(4,128)}, f32[6,3,2,1024]{3,1,2,0:T(4,128)S(1)}, u32[]{:S(2)}, u32[]{:S(2)}) collective-permute-start(f32[6,3,2,1024]{3,1,2,0:T(4,128)} %get-tuple-element.40), channel_id=1, source_target_pairs={{0,1},{1,2},{2,3},{3,0},{4,5},{5,6},{6,7},{7,4},{8,9},{9,10},{10,1... | collective-permute-start | bytes 442376 | tf_op jit(solution)/shard_map/ppermute | solution.py:20
  239.0 14.0 %slice-start.3 = ((s8[6291456]{0:T(1024)(128)(4,1)}), s8[4194304]{0:T(1024)(128)(4,1)S(1)}, s32[]{:S(2)}) async-start(s8[6291456]{0:T(1024)(128)(4,1)} %bitcast.49), calls=%async_computation.4 | async-start | bytes 8388608
  245.3 7.6 %slice-start.4 = ((s8[6291456]{0:T(1024)(128)(4,1)}), s8[2097152]{0:T(1024)(128)(4,1)S(1)}, s32[]{:S(2)}) async-start(s8[6291456]{0:T(1024)(128)(4,1)} %bitcast.49), calls=%async_computation.5 | async-start | bytes 4194304
  306.1 6.4 %collective-permute-start.3 = (bf16[6,1,2,1024]{3,1,2,0:T(2,128)(2,1)S(1)}, bf16[6,1,2,1024]{3,1,2,0:T(2,128)(2,1)S(1)}, u32[]{:S(2)}, u32[]{:S(2)}) collective-permute-start(bf16[6,1,2,1024]{3,1,2,0:T(2,128)(2,1)S(1)} %get-tuple-element.42), channel_id=1, source_target_pairs={{1,0},{2,1},{3,2},{0,3},{5,4},{6,5},{7,6},{4,7},{9,8},{10,9},{11,1... | collective-permute-start | bytes 73736 | tf_op jit(solution)/shard_map/ppermute | solution.py:21
  309.9 5.9 %collective-permute-start.2 = (bf16[6,1,2,1024]{3,1,2,0:T(2,128)(2,1)S(1)}, bf16[6,1,2,1024]{3,1,2,0:T(2,128)(2,1)S(1)}, u32[]{:S(2)}, u32[]{:S(2)}) collective-permute-start(bf16[6,1,2,1024]{3,1,2,0:T(2,128)(2,1)S(1)} %get-tuple-element.41), channel_id=1, source_target_pairs={{0,1},{1,2},{2,3},{3,0},{4,5},{5,6},{6,7},{7,4},{8,9},{9,10},{10,1... | collective-permute-start | bytes 73736 | tf_op jit(solution)/shard_map/ppermute | solution.py:20
Sparse Core Ops, SparseCore 0:
  30.9 174.9 all-reduce.1
where the time goes:
time: 424 us; the launch traced here: 418 us
  other arithmetic  139 us (33%)
  local copies, waits for them, and re-layouts  109 us (26%)
  waiting for transfers between devices  105 us (25%)
  matrix products  40.2 us (9%)
  between operations  16.9 us (4%)
  starting transfers between devices  7.43 us (2%)
    psum x1, waiting for transfers between devices, broadcast(): return lax.psum(kept, axis)  101 us
    broadcast_in_dim x1, other arithmetic, per_device(): return updated[None]  73.8 us
    slice x6, local copies, waits for them, and re-layouts, first_across(): jnp.roll(values, -offset_cells, axis_number)  38.2 us
    dot_general x1, matrix products, along_terms(): jnp.einsum('ij,cjzy->cizy', inverse, compact_rhs, precision=lax.Precision...  37.6 us
    slice x6, local copies, waits for them, and re-layouts, first_across(): jnp.roll(values, offset_cells, axis_number)  24.1 us
    select_n x1, other arithmetic, broadcast(): jnp.where(lax.axis_index(axis) == source, value, 0).astype(value.dtype)  23.5 us
    unnamed x20, local copies, waits for them, and re-layouts  22 us
    concatenate x1, other arithmetic, extended(): array = jnp.concatenate([before, array, after], axis=dim)  14.4 us
  transfers between devices with their start and end apart: 5, of which 2 were waited for; matrix products, arithmetic and copies ran while one was open for 26% of the time, Pallas kernels for 0%

commit v1 on v0

--- a/solution.py
+++ b/solution.py
@@ -25,7 +25,7 @@
 
 def broadcast(value, axis, source):
     kept = jnp.where(lax.axis_index(axis) == source, value, 0).astype(value.dtype)
-    return lax.psum(kept, axis)
+    return jnp.sum(lax.all_gather(kept, axis), axis=0)
 
 
 def first_across(values, axis_number):

time: 424 us -> 740 us (1.75)
  waiting for transfers between devices: 105 us -> 380 us
  local copies, waits for them, and re-layouts: 109 us -> 132 us
  other arithmetic: 139 us -> 160 us
    all_gather x0 -> x1, waiting for transfers between devices: none -> 373 us  [broadcast(): return jnp.sum(lax.all_gather(kept, axis), axis=0)]
    psum x1 -> x0, waiting for transfers between devices: 101 us -> none  [broadcast(): return lax.psum(kept, axis)]
    reduce_sum x0 -> x1, other arithmetic: none -> 38.2 us  [broadcast(): return jnp.sum(lax.all_gather(kept, axis), axis=0)]
    select_n x1, other arithmetic: 23.5 us -> 5.13 us  [broadcast(): jnp.where(lax.axis_index(axis) == source, value, 0).astype(value.dtype)]
    slice x6, local copies, waits for them, and re-layouts: 24.1 us -> 42 us  [first_across(): jnp.roll(values, offset_cells, axis_number)]
    unnamed x20 -> x16, local copies, waits for them, and re-layouts: 22 us -> 29.5 us
  transfers between devices with their start and end apart: 5 -> 5, of which waited for: 2 -> 3; matrix products, arithmetic and copies ran while one was open for 26% -> 11% of each run, Pallas kernels for 0% -> 0%
where the time goes in v1:
time: 740 us; the launch traced here: 736 us
  waiting for transfers between devices  380 us (51%)
  other arithmetic  160 us (22%)
  local copies, waits for them, and re-layouts  132 us (18%)
  matrix products  39.5 us (5%)
  between operations  17.2 us (2%)
    all_gather x1, waiting for transfers between devices, broadcast(): return jnp.sum(lax.all_gather(kept, axis), axis=0)  373 us
    broadcast_in_dim x1, other arithmetic, per_device(): return updated[None]  75.3 us
    slice x6, local copies, waits for them, and re-layouts, first_across(): jnp.roll(values, offset_cells, axis_number)  42 us
    reduce_sum x1, other arithmetic, broadcast(): return jnp.sum(lax.all_gather(kept, axis), axis=0)  38.2 us
    slice x6, local copies, waits for them, and re-layouts, first_across(): jnp.roll(values, -offset_cells, axis_number)  37.5 us
    dot_general x1, matrix products, along_terms(): jnp.einsum('ij,cjzy->cizy', inverse, compact_rhs, precision=lax.Precision...  36.9 us
    unnamed x16, local copies, waits for them, and re-layouts  29.5 us
  transfers between devices with their start and end apart: 5, of which 3 were waited for; matrix products, arithmetic and copies ran while one was open for 11% of the time, Pallas kernels for 0%

profile of v1, /device:TPU:0, one launch (start us, length us, event | category | flops | bytes accessed | tf_op | source)
XLA Modules:
  0.0 736.3 jit_solution(7202969446040693820)
XLA Ops:
  7.2 5.1 broadcast_select_fusion
  12.3 22.9 %copy.21 = f32[1,3,256,8,1024]{4,2,3,1,0:T(8,128)S(1)} copy(f32[1,3,256,8,1024]{4,3,2,1,0:T(8,128)} %param.5) | data formatting | bytes 50331648 | tf_op args[0]
  35.3 4.0 slice.347
  39.3 2.6 fusion.46
  46.1 4.8 fusion.70
  53.8 1.5 fusion.82
  55.3 2.8 slice_bitcast_fusion.2
  58.1 11.1 %fusion.77 = (f32[3,256,2,1023]{3,1,2,0:T(8,128)}, f32[3,256,2,1023]{3,1,2,0:T(8,128)}) fusion(f32[3,256,8,1024]{3,1,2,0:T(8,128)} %bitcast.41), kind=kLoop, calls=%fused_computation.116 | loop fusion | bytes 25141248 | tf_op jit(solution)/shard_map/jit(_roll_static)/slice | solution.py:35
  69.1 11.1 %fusion.79 = (f32[3,256,2,1022]{3,1,2,0:T(8,128)}, f32[3,256,2,1022]{3,1,2,0:T(8,128)}) fusion(f32[3,256,8,1024]{3,1,2,0:T(8,128)} %bitcast.42), kind=kLoop, calls=%fused_computation.118 | loop fusion | bytes 25116672 | tf_op jit(solution)/shard_map/jit(_roll_static)/slice | solution.py:35
  80.2 11.0 %fusion.81 = (f32[3,256,2,1021]{3,1,2,0:T(8,128)}, f32[3,256,2,1021]{3,1,2,0:T(8,128)}) fusion(f32[3,256,8,1024]{3,1,2,0:T(8,128)} %bitcast.43), kind=kLoop, calls=%fused_computation.120 | loop fusion | bytes 25092096 | tf_op jit(solution)/shard_map/jit(_roll_static)/slice | solution.py:35
  91.3 373.2 %all-gather.2.cloned.1.call-done = bf16[8,3,256,8,1024]{4,3,2,1,0:T(8,128)(2,1)} async-done(((bf16[1,3,256,8,1024]{4,3,2,1,0:T(8,128)(2,1)}), bf16[8,3,256,8,1024]{4,3,2,1,0:T(8,128)(2,1)}) %all-gather.2.cloned.1.call-update) | async-done | bytes 100663312 | tf_op jit(solution)/shard_map/all_gather | solution.py:28
  464.5 38.2 %reduce_sum.21 = bf16[3,256,8,1024]{3,2,1,0:T(8,128)(2,1)} reduce(bf16[8,3,256,8,1024]{4,3,2,1,0:T(8,128)(2,1)} %all-gather.2.cloned.1.call-done, bf16[]{:T(256)} %constant.68.clone.1), dimensions={0}, to_apply=%region_0.1 | reduce | flops 44040192 | bytes 113246208 | tf_op jit(solution)/shard_map/reduce_sum | solution.py:28
  502.6 11.4 %copy_convert_fusion = f32[3,256,8,1024]{3,1,2,0:T(8,128)S(1)} fusion(bf16[3,256,8,1024]{3,2,1,0:T(8,128)(2,1)} %reduce_sum.21), kind=kLoop, calls=%fused_computation.11 | loop fusion | flops 6291456 | bytes 37748736 | tf_op jit(solution)/shard_map/convert_element_type | solution.py:126
  514.1 3.6 slice.349
  517.7 6.5 copy-done.1
  524.3 2.9 slice_bitcast_fusion.5
  527.2 11.1 %fusion.84 = (f32[3,256,2,1021]{3,1,2,0:T(8,128)}, f32[3,256,2,1021]{3,1,2,0:T(8,128)}) fusion(f32[3,256,8,1024]{3,1,2,0:T(8,128)} %copy-done.1), kind=kLoop, calls=%fused_computation.123 | loop fusion | bytes 25092096 | tf_op jit(solution)/shard_map/jit(_roll_static)/slice | solution.py:36
  538.3 11.2 %fusion.86 = (f32[3,256,2,1022]{3,1,2,0:T(8,128)}, f32[3,256,2,1022]{3,1,2,0:T(8,128)}) fusion(f32[3,256,8,1024]{3,1,2,0:T(8,128)} %copy-done.1), kind=kLoop, calls=%fused_computation.125 | loop fusion | bytes 25116672 | tf_op jit(solution)/shard_map/jit(_roll_static)/slice | solution.py:36
  549.6 11.2 %fusion.88 = (f32[3,256,2,1023]{3,1,2,0:T(8,128)}, f32[3,256,2,1023]{3,1,2,0:T(8,128)}) fusion(f32[3,256,8,1024]{3,1,2,0:T(8,128)} %copy-done.1), kind=kLoop, calls=%fused_computation.127 | loop fusion | bytes 25141248 | tf_op jit(solution)/shard_map/jit(_roll_static)/slice | solution.py:36
  560.7 3.0 fusion.83
  565.0 3.4 collective-permute-start
  568.3 2.8 fusion.85
  571.1 2.5 collective-permute-done
  573.6 4.5 collective-permute-done.1
  578.1 9.7 %pad_maximum_fusion = (f32[6,259,2,1024]{3,1,2,0:T(8,128)}, f32[6,259,2,1024]{3,1,2,0:T(8,128)}) fusion(f32[6,3,2,1024]{3,1,2,0:T(4,128)S(1)} %collective-permute-done, f32[3,256,2,1024]{3,1,2,0:T(8,128)S(1)} %bitcast.48, f32[3,256,2,1024]{3,1,2,0:T(8,128)S(1)} %bitcast.46, f32[6,3,2,1024]{3,1,2,0:T(4,128)S(1)} %collective-permute-done.1), kind=kLoop, calls=%fused_computation.1 | loop fusion | flops 12730368 | bytes 38338560 | tf_op jit(solution)/shard_map/concatenate | solution.py:22
  587.8 36.9 %fusion.91 = (bf16[6,256,2,1024]{3,1,2,0:T(8,128)(2,1)}, f32[6,256,2,1024]{3,1,2,0:T(8,128)}) fusion(f32[256,256]{0,1:T(8,128)S(1)} %fusion.46, f32[6,259,2,1024]{3,1,2,0:T(8,128)} %get-tuple-element.38, f32[6,259,2,1024]{3,1,2,0:T(8,128)} %get-tuple-element.37), kind=kOutput, calls=%fused_computation.130 | convolution fusion | flops 9682550784 | bytes 69468160 | tf_op jit(solution)/shard_map/ij,cjzy->cizy/dot_general | solution.py:92
  625.8 1.6 collective-permute-start.2
  627.4 2.3 collective-permute-start.3
  629.7 2.8 fusion.87
  633.8 12.5 %multiply_subtract_fusion = f32[6,256,2,1024]{3,1,2,0:T(8,128)} fusion(f32[6,256,2,1024]{3,1,2,0:T(8,128)} %get-tuple-element.46, f32[6,2,1024]{2,1,0:T(2,128)S(1)} %get-tuple-element.47, f32[256]{0:T(256)S(1)} %bitcast.50, f32[6,2,1024]{2,1,0:T(2,128)S(1)} %get-tuple-element.48, f32[256]{0:T(256)S(1)} %bitcast.49), kind=kLoop, calls=%fused_computation.12 | loop fusion | flops 15728640 | bytes 25266176 | tf_op jit(solution)/shard_map/sub | solution.py:106
  646.3 75.3 %fusion.16 = f32[1,3,256,2,1024]{4,2,3,1,0:T(8,128)S(1)} fusion(f32[6,259,2,1024]{3,1,2,0:T(8,128)} %get-tuple-element.38, f32[6,259,2,1024]{3,1,2,0:T(8,128)} %get-tuple-element.37, f32[3,256,8,1024]{3,1,2,0:T(8,128)} %copy-done.1, f32[6,256,2,1024]{3,1,2,0:T(8,128)} %multiply_subtract_fusion, f32[3,256,2,1]{3,1,2,0:T(8,128)} %get-tuple-element.32, ...), kind=kLoop, calls=%fused_computation.23 | loop fusion | flops 141557760 | bytes 226492416 | tf_op jit(solution)/shard_map/broadcast_in_dim | solution.py:141
  721.6 7.6 %copy.12 = f32[1,3,256,2,1024]{4,3,2,1,0:T(2,128)} copy(f32[1,3,256,2,1024]{4,2,3,1,0:T(8,128)S(1)} %fusion.16) | data formatting | bytes 12582912 | tf_op jit(solution)/shard_map/broadcast_in_dim | solution.py:141
  (30 shorter events, 8.0 us)
Async XLA Ops:
  6.5 457.9 %all-gather.2.cloned.1.call-start = ((), (), s32[]{:S(2)}) async-start(), calls=%async_computation | async-start | bytes 113246208 | tf_op jit(solution)/shard_map/all_gather | solution.py:28
  35.3 20.0 %copy-start = (f32[1,3,256,8,1024]{4,2,3,1,0:T(8,128)}, f32[1,3,256,8,1024]{4,2,3,1,0:T(8,128)S(1)}, u32[]{:S(2)}) copy-start(f32[1,3,256,8,1024]{4,2,3,1,0:T(8,128)S(1)} %copy.21) | copy-start | bytes 75497472
  35.3 10.9 %copy-start.2 = (f32[64]{0:T(128)S(1)}, f32[64]{0:T(128)}, u32[]{:S(2)}) copy-start(f32[64]{0:T(128)} %param.9) | copy-start | bytes 772
  514.1 10.2 %copy-start.1 = (f32[3,256,8,1024]{3,1,2,0:T(8,128)}, f32[3,256,8,1024]{3,1,2,0:T(8,128)S(1)}, u32[]{:S(2)}) copy-start(f32[3,256,8,1024]{3,1,2,0:T(8,128)S(1)} %copy_convert_fusion) | copy-start | bytes 75497472
  538.3 25.4 %slice-start = ((s8[6291456]{0:T(1024)(128)(4,1)}), s8[4194304]{0:T(1024)(128)(4,1)S(1)}, s32[]{:S(2)}) async-start(s8[6291456]{0:T(1024)(128)(4,1)} %bitcast.45), calls=%async_computation.1 | async-start | bytes 8388608
  549.6 14.1 %slice-start.1 = ((s8[6291456]{0:T(1024)(128)(4,1)}), s8[2097152]{0:T(1024)(128)(4,1)S(1)}, s32[]{:S(2)}) async-start(s8[6291456]{0:T(1024)(128)(4,1)} %bitcast.45), calls=%async_computation.2 | async-start | bytes 4194304
  560.7 17.4 %slice-start.2 = ((s8[6291456]{0:T(1024)(128)(4,1)}), s8[4194304]{0:T(1024)(128)(4,1)S(1)}, s32[]{:S(2)}) async-start(s8[6291456]{0:T(1024)(128)(4,1)} %bitcast.47), calls=%async_computation.3 | async-start | bytes 8388608
  563.7 14.4 %slice-start.3 = ((s8[6291456]{0:T(1024)(128)(4,1)}), s8[2097152]{0:T(1024)(128)(4,1)S(1)}, s32[]{:S(2)}) async-start(s8[6291456]{0:T(1024)(128)(4,1)} %bitcast.47), calls=%async_computation.4 | async-start | bytes 4194304
  565.0 8.7 %collective-permute-start = (f32[6,3,2,1024]{3,1,2,0:T(4,128)S(1)}, f32[6,3,2,1024]{3,1,2,0:T(4,128)S(1)}, u32[]{:S(2)}, u32[]{:S(2)}) collective-permute-start(f32[6,3,2,1024]{3,1,2,0:T(4,128)S(1)} %get-tuple-element.39), channel_id=1, source_target_pairs={{1,0},{2,1},{3,2},{0,3},{5,4},{6,5},{7,6},{4,7},{9,8},{10,9},{11,1... | collective-permute-start | bytes 442376 | tf_op jit(solution)/shard_map/ppermute | solution.py:21
  568.3 9.8 %collective-permute-start.1 = (f32[6,3,2,1024]{3,1,2,0:T(4,128)S(1)}, f32[6,3,2,1024]{3,1,2,0:T(4,128)S(1)}, u32[]{:S(2)}, u32[]{:S(2)}) collective-permute-start(f32[6,3,2,1024]{3,1,2,0:T(4,128)S(1)} %get-tuple-element.40), channel_id=1, source_target_pairs={{0,1},{1,2},{2,3},{3,0},{4,5},{5,6},{6,7},{7,4},{8,9},{9,10},{10,1... | collective-permute-start | bytes 442376 | tf_op jit(solution)/shard_map/ppermute | solution.py:20
  625.8 6.7 collective-permute-start.2
  627.4 5.1 collective-permute-start.3
Sparse Core Ops, SparseCore 0:
  12.5 451.9 all-gather.1
